TPU v7x, 128 devices: a whole 4x4x4 slice. The times are simulated.
128 devices in a mesh: grp: 4 (over y_lo, core), mem: 32 (over x, y_hi, z).
Axes of the slice: x: 4, y: 4 (y_hi: 2, y_lo: 2; y = y_hi * 2 + y_lo), z: 4, core: 2. Of those that a mesh axis runs over, the one named last changes fastest.
Arguments:
- amplitudes: float32 [192, 4, 32, 2000], P('mem', 'grp'), may hold values from -6 to 6
- singles: float32 [250, 2000], replicated, may hold values from -5 to 5
- pair_list: int32 [192, 2], replicated, may hold values from 0 to 249, as said below
- mirror: int32 [192], replicated, may hold values from 0 to 191, as said below
- slab_rows: int32 [2048, 2], P('grp'), may hold values from 0 to 1999
- occ_energy: float32 [250], replicated, may hold values from -1 to -0.2
- vir_energy: float32 [2000], replicated, may hold values from 0.2 to 1
- integrals: float32 [2048, 4, 32, 2000], P('grp', None, 'mem'), may hold values from -0.01171875 to 0.01171875
Outputs:
- update: float32 [192, 2048], P('mem', 'grp')
Inputs may be any that keep to these rules, and one draw needn't show every extreme that they name: `pair_list`: each row holds two occupied orbitals i < j; no pair appears twice. mirror[mirror[p]] = p and mirror[p] != p; a pair p of owner block k = p // 6 is mapped into owner block (k + 32 / 2) mod 32.
All inputs are finite; a program needn't handle non-finite values.
Results may differ from a plain program's by a relative error of at most 0.000073.
Values sent between devices are 32-bit elements; how exact they have to be, the bound alone decides.
No kernel may reach another device: no remote copies, remote signals or barrier semaphores. Data moves between devices by JAX's collectives and lax.ppermute only.
A program may use at most 128 MiB of HBM per device.

v0:
```python
import jax
import jax.numpy as jnp
from jax import lax
from jax.sharding import PartitionSpec as P


def shifted(block, axis, distance):
    devices = range(lax.axis_size(axis))
    route = [((i - distance) % len(devices), i) for i in devices]
    return lax.ppermute(block, axis, route)


def body(amplitudes, singles, pair_list, mirror, slab_rows, occ_energy, vir_energy, integrals):
    owners = lax.axis_size("mem")
    member = lax.axis_index("mem")
    pair_dev = amplitudes.shape[0]
    pair_total = pair_dev * owners
    partner = shifted(amplitudes, "mem", owners // 2)
    own_mirror = lax.dynamic_slice_in_dim(mirror, member * pair_dev, pair_dev, 0)
    local_slot = own_mirror % pair_dev
    prepared = amplitudes - jnp.take(partner, local_slot, axis=0)
    quarters = lax.all_gather(prepared, "grp", axis=1, tiled=True)
    regrouped = lax.all_to_all(quarters, "mem", split_axis=2, concat_axis=0, tiled=True)
    group_count = regrouped.shape[1]
    block_len = regrouped.shape[2]
    block_full = block_len * owners
    first_rows = jnp.take(singles, pair_list[:, 0], axis=0)
    second_rows = jnp.take(singles, pair_list[:, 1], axis=0)

    def window(orbital_rows):
        columns = orbital_rows[:, : group_count * block_full].reshape(
            pair_total, group_count, block_full
        )
        return lax.dynamic_slice_in_dim(columns, member * block_len, block_len, 2)

    first_window = window(first_rows)
    second_window = window(second_rows)
    tau_full = (
        regrouped
        + first_window[:, :, :, None] * second_rows[:, None, None, :]
        - second_window[:, :, :, None] * first_rows[:, None, None, :]
    )
    flat_tau = tau_full.reshape(pair_total, -1)
    flat_ints = integrals.reshape(integrals.shape[0], -1)
    summed = lax.psum_scatter(
        0.5
        * lax.dot_general(
            flat_tau,
            flat_ints,
            (((1,), (1,)), ((), ())),
            precision=lax.Precision.HIGHEST,
            preferred_element_type=jnp.float32,
        ),
        "mem",
        scatter_dimension=0,
        tiled=True,
    )
    own_pairs = lax.dynamic_slice_in_dim(pair_list, member * pair_dev, pair_dev, 0)
    occ_first = jnp.take(occ_energy, own_pairs[:, 0])
    occ_second = jnp.take(occ_energy, own_pairs[:, 1])
    vir_first = jnp.take(vir_energy, slab_rows[:, 0])
    vir_second = jnp.take(vir_energy, slab_rows[:, 1])
    denominator = (
        vir_first[None, :] + vir_second[None, :] - occ_first[:, None] - occ_second[:, None]
    )
    return summed / denominator


def solution(mesh):
    in_specs = (
        P("mem", "grp", None, None),
        P(),
        P(),
        P(),
        P("grp", None),
        P(),
        P(),
        P("grp", None, "mem", None),
    )
    out_specs = P("mem", "grp")
    return jax.shard_map(body, mesh=mesh, in_specs=in_specs, out_specs=out_specs, check_vma=False)
```

profile of v0, /device:TPU:120, one launch (start us, length us, event | category | flops | bytes accessed | tf_op | source)
XLA Modules:
  0.0 454.6 jit_solution(17607641296579111596)
XLA Ops:
  6.5 0.0 copy-start
  6.5 0.0 all-gather.2.cloned.1.call-start
  6.5 3.0 collective-permute-start
  9.6 0.8 compare_and_fusion.2
  10.3 34.0 %collective-permute-done = f32[6,1,32,2000]{3,2,0,1:T(8,128)S(1)} collective-permute-done((f32[6,1,32,2000]{3,2,0,1:T(8,128)}, f32[6,1,32,2000]{3,2,0,1:T(8,128)S(1)}, u32[]{:S(2)}, u32[]{:S(2)}) %collective-permute-start) | collective-permute-done | bytes 1536032 | tf_op jit(solution)/shard_map/ppermute | solution.py:10
  44.4 1.2 copy-done.5
  45.5 2.1 gather_fusion
  47.6 0.0 copy-done.4
  47.6 1.4 fusion.5
  49.0 0.0 all-gather.2.cloned.1.call-update
  49.1 63.4 %all-gather.2.cloned.1.call-done = f32[6,4,32,2000]{3,2,0,1:T(8,128)} async-done(((f32[6,1,32,2000]{3,2,0,1:T(8,128)}), f32[6,4,32,2000]{3,2,0,1:T(8,128)}) %all-gather.2.cloned.1.call-update) | async-done | bytes 6144016 | tf_op jit(solution)/shard_map/all_gather | solution.py:22
  112.5 9.8 %copy.43 = f32[6,4,32,2000]{3,0,1,2:T(8,128)} copy(f32[6,4,32,2000]{3,2,0,1:T(8,128)} %all-gather.2.cloned.1.call-done) | data formatting | bytes 12288000 | tf_op jit(solution)/shard_map/all_gather | solution.py:22
  122.2 9.8 %all-to-all-start = ((f32[6,4,32,2000]{3,0,1,2:T(8,128)}), f32[6,4,32,2000]{3,0,1,2:T(8,128)}, u32[]{:S(2)}, u32[]{:S(2)}) async-start(f32[6,4,32,2000]{3,0,1,2:T(8,128)} %copy.43), calls=%async_computation | async-start | bytes 16777216 | tf_op jit(solution)/shard_map/all_to_all | solution.py:23
  132.0 0.0 copy-start.6
  132.0 1.9 copy.44
  133.9 0.0 copy-done.6
  134.0 2.3 gather_fusion.2
  136.3 1.6 broadcast_select_fusion
  137.9 0.0 copy-start.3
  137.9 1.2 copy-done.3
  139.1 2.7 mul.67
  141.8 2.3 gather_fusion.1
  144.1 1.6 broadcast_select_fusion.1
  145.7 0.0 slice-start
  145.7 0.0 copy-start.7
  145.7 1.5 mul.72
  147.2 0.1 copy.45
  147.4 0.1 mul.65
  147.5 0.0 slice-done
  147.5 0.1 copy.48
  147.7 0.1 mul.70
  147.8 0.0 copy-done.7
  147.9 0.0 copy-done
  147.9 0.0 copy-start.2
  147.9 3.1 gather_fusion.4
  151.1 3.1 gather_fusion.3
  154.2 0.1 constant_dynamic-slice_fusion
  154.3 120.5 %all-to-all-done = f32[6,4,32,2000]{3,0,1,2:T(8,128)} async-done(((f32[6,4,32,2000]{3,0,1,2:T(8,128)}), f32[6,4,32,2000]{3,0,1,2:T(8,128)}, u32[]{:S(2)}, u32[]{:S(2)}) %all-to-all-start) | async-done | bytes 6144032 | tf_op jit(solution)/shard_map/all_to_all | solution.py:23
  274.9 4.9 %fusion.3 = f32[32,6,4,1,2000]{4,1,2,0,3:T(8,128)S(1)} fusion(f32[6,4,32,2000]{3,0,1,2:T(8,128)} %all-to-all-done, f32[32,6,2000]{2,1,0:T(8,128)} %mul.72, f32[32,6,4]{1,2,0:T(4,128)S(1)} %copy.49, f32[32,6,2000]{2,1,0:T(8,128)S(1)} %copy-done.2, f32[32,6,4]{1,2,0:T(4,128)S(1)} %copy.46), kind=kLoop, calls=%fused_computation.10 | loop fusion | flops 6144000 | bytes 15366144 | tf_op jit(solution)/shard_map/sub | solution.py:39
  279.8 8.1 %copy.50 = f32[32,6,4,1,2000]{4,2,1,0,3:T(4,128)} copy(f32[32,6,4,1,2000]{4,1,2,0,3:T(8,128)S(1)} %fusion.3) | data formatting | bytes 12288000 | tf_op jit(solution)/shard_map/sub | solution.py:39
  287.8 19.3 %fusion.11 = f32[192,512]{1,0:T(8,128)S(1)} fusion(f32[512,4,1,2000]{0,3,2,1:T(8,128)} %param.21, f32[192,4,2000]{2,1,0:T(4,128)} %bitcast.47), kind=kOutput, calls=%fused_computation.15 | convolution fusion | flops 9437282304 | bytes 22921216 | tf_op jit(solution)/shard_map/dot_general | solution.py:47
  307.1 86.3 %fusion = f32[8,512]{1,0:T(8,128)S(1)} fusion(f32[192,512]{1,0:T(8,128)S(1)} %fusion.11), kind=kCustom, calls=%all-reduce-scatter | all-reduce-scatter fusion | flops 131073 | bytes 410112
  393.5 8.2 %collective-permute-start.1 = (f32[8,512]{1,0:T(8,128)S(1)}, f32[8,512]{1,0:T(8,128)S(1)}, u32[]{:S(2)}, u32[]{:S(2)}) collective-permute-start(f32[8,512]{1,0:T(8,128)S(1)} %fusion), channel_id=1, source_target_pairs={{0,1},{1,2},{2,3},{3,4},{4,5},{5,6},{6,7},{7,8},{8,9},{9,10},{10,1... | collective-permute-start | bytes 49160
  401.7 1.9 collective-permute-start.2
  403.7 13.4 %collective-permute-start.8 = (f32[6,512]{1,0:T(8,128)S(1)}, f32[6,512]{1,0:T(8,128)S(1)}, u32[]{:S(2)}, u32[]{:S(2)}) collective-permute-start(f32[6,512]{1,0:T(8,128)S(1)} %slice.48), channel_id=1, source_target_pairs={{0,8},{1,9},{2,10},{3,11},{4,12},{5,13},{6,14},{7,15},{8,16},{9,17... | collective-permute-start | bytes 36872
  417.0 0.0 copy-done.1
  417.0 0.6 gather_fusion.5
  417.7 0.6 gather_fusion.6
  418.3 1.9 collective-permute-start.3
  420.3 5.2 %collective-permute-start.4 = (f32[8,512]{1,0:T(8,128)S(1)}, f32[8,512]{1,0:T(8,128)S(1)}, u32[]{:S(2)}, u32[]{:S(2)}) collective-permute-start(f32[8,512]{1,0:T(8,128)S(1)} %fusion), channel_id=1, source_target_pairs={{0,4},{1,5},{2,6},{3,7},{4,8},{5,9},{6,10},{7,11},{8,12},{9,13},{1... | collective-permute-start | bytes 49160
  425.4 0.0 collective-permute-done.8
  425.5 5.5 %collective-permute-start.5 = (f32[8,512]{1,0:T(8,128)S(1)}, f32[8,512]{1,0:T(8,128)S(1)}, u32[]{:S(2)}, u32[]{:S(2)}) collective-permute-start(f32[8,512]{1,0:T(8,128)S(1)} %fusion), channel_id=1, source_target_pairs={{0,5},{1,6},{2,7},{3,8},{4,9},{5,10},{6,11},{7,12},{8,13},{9,14},{... | collective-permute-start | bytes 49160
  431.0 0.0 collective-permute-done.1
  431.0 6.0 %collective-permute-start.6 = (f32[8,512]{1,0:T(8,128)S(1)}, f32[8,512]{1,0:T(8,128)S(1)}, u32[]{:S(2)}, u32[]{:S(2)}) collective-permute-start(f32[8,512]{1,0:T(8,128)S(1)} %fusion), channel_id=1, source_target_pairs={{0,6},{1,7},{2,8},{3,9},{4,10},{5,11},{6,12},{7,13},{8,14},{9,15},... | collective-permute-start | bytes 49160
  437.1 0.0 collective-permute-done.2
  437.1 1.9 collective-permute-start.7
  439.0 0.6 dynamic-slice.4
  440.3 0.0 collective-permute-done.3
  440.3 0.0 collective-permute-done.4
  440.3 0.0 collective-permute-done.5
  440.3 0.3 collective-permute-done.6
  440.5 5.8 %collective-permute-done.7 = f32[8,512]{1,0:T(8,128)S(1)} collective-permute-done((f32[8,512]{1,0:T(8,128)S(1)}, f32[8,512]{1,0:T(8,128)S(1)}, u32[]{:S(2)}, u32[]{:S(2)}) %collective-permute-start.7) | collective-permute-done | bytes 16416
  446.3 0.8 concatenate
  447.1 0.7 dynamic-slice_divide_fusion
  (27 shorter events, 0.3 us)
Async XLA Ops:
  6.5 141.4 %copy-start = (f32[2000]{0:T(1024)S(1)}, f32[2000]{0:T(1024)}, u32[]{:S(2)}) copy-start(f32[2000]{0:T(1024)} %param.20) | copy-start | bytes 24004
  6.5 41.1 %copy-start.4 = (f32[6,1,32,2000]{3,2,1,0:T(8,128)S(1)}, f32[6,1,32,2000]{3,2,1,0:T(8,128)}, u32[]{:S(2)}) copy-start(f32[6,1,32,2000]{3,2,1,0:T(8,128)} %param.14) | copy-start | bytes 4608004
  6.5 105.9 %all-gather.2.cloned.1.call-start = ((), (), s32[]{:S(2)}) async-start(), calls=%async_computation.1 | async-start | bytes 7864320 | tf_op jit(solution)/shard_map/all_gather | solution.py:22
  6.5 37.8 %collective-permute-start = (f32[6,1,32,2000]{3,2,0,1:T(8,128)}, f32[6,1,32,2000]{3,2,0,1:T(8,128)S(1)}, u32[]{:S(2)}, u32[]{:S(2)}) collective-permute-start(f32[6,1,32,2000]{3,2,0,1:T(8,128)} %bitcast.48), channel_id=1, source_target_pairs={{16,0},{17,1},{18,2},{19,3},{20,4},{21,5},{22,6},{23,7},{24,8},{25... | collective-permute-start | bytes 4608008 | tf_op jit(solution)/shard_map/ppermute | solution.py:10
  44.4 1.2 copy-start.5
  122.2 152.6 %all-to-all-start = ((f32[6,4,32,2000]{3,0,1,2:T(8,128)}), f32[6,4,32,2000]{3,0,1,2:T(8,128)}, u32[]{:S(2)}, u32[]{:S(2)}) async-start(f32[6,4,32,2000]{3,0,1,2:T(8,128)} %copy.43), calls=%async_computation | async-start | bytes 16777216 | tf_op jit(solution)/shard_map/all_to_all | solution.py:23
  132.0 1.9 copy-start.6
  137.9 1.2 copy-start.3
  145.7 1.8 slice-start
  145.7 2.1 copy-start.7
  147.9 127.0 %copy-start.2 = (f32[32,6,2000]{2,1,0:T(8,128)S(1)}, f32[32,6,2000]{2,1,0:T(8,128)}, u32[]{:S(2)}) copy-start(f32[32,6,2000]{2,1,0:T(8,128)} %mul.67) | copy-start | bytes 4608004
  287.8 129.2 %copy-start.1 = (f32[250]{0:T(256)S(1)}, f32[250]{0:T(256)}, u32[]{:S(2)}) copy-start(f32[250]{0:T(256)} %param.19) | copy-start | bytes 3004
  287.8 151.2 %copy-start.8 = (u32[128]{0:T(128)S(1)}, u32[128]{0:T(128)}, u32[]{:S(2)}) copy-start(u32[128]{0:T(128)} %constant.71) | copy-start | bytes 1540
  393.5 37.5 %collective-permute-start.1 = (f32[8,512]{1,0:T(8,128)S(1)}, f32[8,512]{1,0:T(8,128)S(1)}, u32[]{:S(2)}, u32[]{:S(2)}) collective-permute-start(f32[8,512]{1,0:T(8,128)S(1)} %fusion), channel_id=1, source_target_pairs={{0,1},{1,2},{2,3},{3,4},{4,5},{5,6},{6,7},{7,8},{8,9},{9,10},{10,1... | collective-permute-start | bytes 49160
  401.7 35.3 %collective-permute-start.2 = (f32[8,512]{1,0:T(8,128)S(1)}, f32[8,512]{1,0:T(8,128)S(1)}, u32[]{:S(2)}, u32[]{:S(2)}) collective-permute-start(f32[8,512]{1,0:T(8,128)S(1)} %fusion), channel_id=1, source_target_pairs={{0,2},{1,3},{2,4},{3,5},{4,6},{5,7},{6,8},{7,9},{8,10},{9,11},{10,... | collective-permute-start | bytes 49160
  403.7 21.8 %collective-permute-start.8 = (f32[6,512]{1,0:T(8,128)S(1)}, f32[6,512]{1,0:T(8,128)S(1)}, u32[]{:S(2)}, u32[]{:S(2)}) collective-permute-start(f32[6,512]{1,0:T(8,128)S(1)} %slice.48), channel_id=1, source_target_pairs={{0,8},{1,9},{2,10},{3,11},{4,12},{5,13},{6,14},{7,15},{8,16},{9,17... | collective-permute-start | bytes 36872
  418.3 21.9 %collective-permute-start.3 = (f32[8,512]{1,0:T(8,128)S(1)}, f32[8,512]{1,0:T(8,128)S(1)}, u32[]{:S(2)}, u32[]{:S(2)}) collective-permute-start(f32[8,512]{1,0:T(8,128)S(1)} %fusion), channel_id=1, source_target_pairs={{0,3},{1,4},{2,5},{3,6},{4,7},{5,8},{6,9},{7,10},{8,11},{9,12},{10... | collective-permute-start | bytes 49160
  420.3 20.0 %collective-permute-start.4 = (f32[8,512]{1,0:T(8,128)S(1)}, f32[8,512]{1,0:T(8,128)S(1)}, u32[]{:S(2)}, u32[]{:S(2)}) collective-permute-start(f32[8,512]{1,0:T(8,128)S(1)} %fusion), channel_id=1, source_target_pairs={{0,4},{1,5},{2,6},{3,7},{4,8},{5,9},{6,10},{7,11},{8,12},{9,13},{1... | collective-permute-start | bytes 49160
  425.5 14.8 %collective-permute-start.5 = (f32[8,512]{1,0:T(8,128)S(1)}, f32[8,512]{1,0:T(8,128)S(1)}, u32[]{:S(2)}, u32[]{:S(2)}) collective-permute-start(f32[8,512]{1,0:T(8,128)S(1)} %fusion), channel_id=1, source_target_pairs={{0,5},{1,6},{2,7},{3,8},{4,9},{5,10},{6,11},{7,12},{8,13},{9,14},{... | collective-permute-start | bytes 49160
  431.0 9.5 %collective-permute-start.6 = (f32[8,512]{1,0:T(8,128)S(1)}, f32[8,512]{1,0:T(8,128)S(1)}, u32[]{:S(2)}, u32[]{:S(2)}) collective-permute-start(f32[8,512]{1,0:T(8,128)S(1)} %fusion), channel_id=1, source_target_pairs={{0,6},{1,7},{2,8},{3,9},{4,10},{5,11},{6,12},{7,13},{8,14},{9,15},... | collective-permute-start | bytes 49160
  437.1 9.2 %collective-permute-start.7 = (f32[8,512]{1,0:T(8,128)S(1)}, f32[8,512]{1,0:T(8,128)S(1)}, u32[]{:S(2)}, u32[]{:S(2)}) collective-permute-start(f32[8,512]{1,0:T(8,128)S(1)} %fusion), channel_id=1, source_target_pairs={{0,7},{1,8},{2,9},{3,10},{4,11},{5,12},{6,13},{7,14},{8,15},{9,16}... | collective-permute-start | bytes 49160
Sparse Core Ops, SparseCore 0:
  49.2 63.2 all-gather.1
where the time goes:
time: 455 us
  waiting for transfers between devices  224 us (49%)
  blocking collectives  86.3 us (19%)
  starting transfers between devices  56.9 us (13%)
  local copies, waits for them, and re-layouts  42.6 us (9%)
  matrix products  19.3 us (4%)
  between operations  14.5 us (3%)
  other arithmetic  11 us (2%)
    all_to_all x1, waiting for transfers between devices, body(): lax.all_to_all(quarters, 'mem', split_axis=2, concat_axis=0, tiled=True)  121 us
    unnamed x1, blocking collectives  86.3 us
    all_gather x1, waiting for transfers between devices, body(): quarters = lax.all_gather(prepared, 'grp', axis=1, tiled=True)  63.4 us
    unnamed x8, starting transfers between devices  44.1 us
    ppermute x1, waiting for transfers between devices, shifted(): return lax.ppermute(block, axis, route)  34 us
    dot_general x1, matrix products, body(): lax.dot_general(flat_tau, flat_ints, (((1,), (1,)), ((), ())), precision=...  19.3 us
    all_gather x1, local copies, waits for them, and re-layouts, body(): quarters = lax.all_gather(prepared, 'grp', axis=1, tiled=True)  9.78 us
    all_to_all x1, starting transfers between devices, body(): lax.all_to_all(quarters, 'mem', split_axis=2, concat_axis=0, tiled=True)  9.76 us
  transfers between devices with their start and end apart: 11, of which 5 were waited for; matrix products, arithmetic and copies ran while one was open for 5% of the time, Pallas kernels for 0%

commit v1 on v0

v1 whole, which is shorter than its diff:
```python
import functools

import jax
import jax.numpy as jnp
from jax import lax
from jax.experimental import pallas as pl
from jax.experimental.pallas import tpu as pltpu
from jax.sharding import PartitionSpec as P

LANES = 128
BF16 = jnp.bfloat16
F32 = jnp.float32


def split(value):
    high = value.astype(BF16)
    return high, (value - high.astype(F32)).astype(BF16)


def pack_kernel(stored_ref, packed_ref, *, chunks):
    offsets, width = stored_ref.shape[2:]
    flat = packed_ref.reshape(offsets * chunks, LANES)
    for first in range(0, offsets, 8):
        for k in range(chunks):
            size = min(LANES, width - k * LANES)
            tile = stored_ref[0, 0, first : first + 8, k * LANES : k * LANES + size]
            if size < LANES:
                tile = jnp.concatenate([tile, jnp.zeros((8, LANES - size), F32)], axis=1)
            flat[pl.ds(first * chunks + k, 8, stride=chunks), :] = tile


def pack(stored, chunks):
    pairs, _, offsets, width = stored.shape
    return pl.pallas_call(
        functools.partial(pack_kernel, chunks=chunks),
        grid=(pairs,),
        in_specs=[pl.BlockSpec((1, 1, offsets, width), lambda p: (p, 0, 0, 0))],
        out_specs=pl.BlockSpec((offsets, chunks, LANES), lambda p: (0, p, 0)),
        out_shape=jax.ShapeDtypeStruct((offsets, pairs * chunks, LANES), F32),
        name="pack",
    )(stored)


def unpack_kernel(mirror_ref, blocks_ref, out_ref):
    def step(p, _):
        out_ref[p] = blocks_ref[p] - blocks_ref[mirror_ref[p]]
        return 0

    lax.fori_loop(0, out_ref.shape[0], step, 0, unroll=8)


def unpack(mirror, blocks):
    pairs, chunks, lanes = blocks.shape
    return pl.pallas_call(
        unpack_kernel,
        in_specs=[pl.BlockSpec(memory_space=pltpu.SMEM), pl.BlockSpec(memory_space=pltpu.VMEM)],
        out_specs=pl.BlockSpec(memory_space=pltpu.VMEM),
        out_shape=jax.ShapeDtypeStruct((pairs // 2, chunks, lanes), F32),
        name="unpack",
    )(mirror, blocks)


def early_kernel(member_ref, first_ref, second_ref, ints_ref, singles_ref, high_ref, low_ref, lhs):
    q = pl.program_id(0)
    pairs, width = first_ref.shape
    padded = lhs.shape[1]

    @pl.when(q == 0)
    def _():
        lhs[:, width // LANES * LANES :] = jnp.zeros((2 * pairs, padded - width // LANES * LANES), BF16)

    high, low = split(ints_ref[0])
    high_ref[0, :width] = high
    low_ref[0, :width] = low
    tail = jnp.zeros((padded - width, high.shape[1]), BF16)
    high_ref[0, width:] = tail
    low_ref[0, width:] = tail

    lane = lax.broadcasted_iota(jnp.int32, (pairs, LANES), 1)
    chosen = lane == q * 32 + member_ref[0]
    first_c = jnp.sum(jnp.where(chosen, first_ref[:, :LANES], 0.0), axis=1, keepdims=True)
    second_c = jnp.sum(jnp.where(chosen, second_ref[:, :LANES], 0.0), axis=1, keepdims=True)
    for start in range(0, width, LANES):
        size = min(LANES, width - start)
        at = slice(start, start + size)
        part = first_c * second_ref[:, at] - second_c * first_ref[:, at]
        part_high, part_low = split(part)
        lhs[:pairs, at] = part_high
        lhs[pairs:, at] = part_low
    both = jnp.dot(lhs[...], high_ref[0], preferred_element_type=F32)
    total = both[:pairs] + both[pairs:]
    total += jnp.dot(lhs[:pairs], low_ref[0], preferred_element_type=F32)

    @pl.when(q == 0)
    def _():
        singles_ref[...] = total

    @pl.when(q > 0)
    def _():
        singles_ref[...] += total


def early(member, first, second, ints, padded):
    pairs, width = first.shape
    quarters, _, rows = ints.shape
    whole = lambda q: (0, 0)
    return pl.pallas_call(
        early_kernel,
        grid=(quarters,),
        in_specs=[
            pl.BlockSpec(memory_space=pltpu.SMEM),
            pl.BlockSpec((pairs, width), whole),
            pl.BlockSpec((pairs, width), whole),
            pl.BlockSpec((1, width, rows), lambda q: (q, 0, 0)),
        ],
        out_specs=[
            pl.BlockSpec((pairs, rows), whole),
            pl.BlockSpec((1, padded, rows), lambda q: (q, 0, 0)),
            pl.BlockSpec((1, padded, rows), lambda q: (q, 0, 0)),
        ],
        out_shape=[
            jax.ShapeDtypeStruct((pairs, rows), F32),
            jax.ShapeDtypeStruct((quarters, padded, rows), BF16),
            jax.ShapeDtypeStruct((quarters, padded, rows), BF16),
        ],
        scratch_shapes=[pltpu.VMEM((2 * pairs, padded), BF16)],
        name="early",
    )(member, first, second, ints)


def fill(lhs, values_ref):
    pairs, chunks, _ = values_ref.shape
    flat = values_ref.reshape(pairs * chunks, LANES)
    for first in range(0, pairs, 16):
        for k in range(chunks):
            tile = flat[pl.ds(first * chunks + k, 16, stride=chunks), :]
            high, low = split(tile)
            at = slice(k * LANES, (k + 1) * LANES)
            lhs[first : first + 16, at] = high
            lhs[pairs + first : pairs + first + 16, at] = low


def product(lhs, high, low):
    pairs = lhs.shape[0] // 2
    both = jnp.dot(lhs[...], high, preferred_element_type=F32)
    return both[:pairs] + both[pairs:] + jnp.dot(lhs[:pairs], low, preferred_element_type=F32)


def contract_kernel(order_ref, *refs, count, has_sum, last):
    values, rest = refs[:count], refs[count:]
    high_ref, low_ref, *rest = rest
    pairs = values[0].shape[0]
    step = pl.program_id(0)
    if has_sum:
        sum_ref, *rest = rest
    if last:
        singles_ref, *rest = rest
    out_ref, lhs, total_ref = rest

    for n in range(count):

        @pl.when(step == n)
        def _(n=n):
            fill(lhs, values[n])

    part = product(lhs, high_ref[0], low_ref[0])
    start = sum_ref[...] if has_sum else jnp.zeros_like(part)
    total = jnp.where(step == 0, start, total_ref[...]) + part if count > 1 else start + part
    if count > 1:
        total_ref[...] = total

    @pl.when(step == count - 1)
    def _():
        if not last:
            out_ref[...] = total
        else:
            rows = total.shape[1]
            per = rows // LANES
            for side in range(2):
                mine = singles_ref[side * pairs : (side + 1) * pairs]
                full = 0.5 * (mine + total if side == 0 else mine - total)
                for first in range(0, pairs, 8):
                    for n in range(per):
                        at = pl.ds((side * pairs + first) * per + n, 8, stride=per)
                        out_ref[at, :] = full[first : first + 8, n * LANES : (n + 1) * LANES]


def contract(order, values, high, low, total=None, singles=None):
    count = len(values)
    pairs, chunks, _ = values[0].shape
    _, padded, rows = high.shape
    vmem = lambda a: pl.BlockSpec(a.shape, lambda n, order: (0,) * a.ndim)
    extra = [a for a in (total, singles) if a is not None]
    part = pl.BlockSpec((1, padded, rows), lambda n, order: (order[n], 0, 0))
    out = (pairs, rows) if singles is None else (2 * pairs * rows // LANES, LANES)
    return pl.pallas_call(
        functools.partial(contract_kernel, count=count, has_sum=total is not None, last=singles is not None),
        grid_spec=pltpu.PrefetchScalarGridSpec(
            num_scalar_prefetch=1,
            grid=(count,),
            in_specs=[vmem(v) for v in values] + [part, part] + [vmem(a) for a in extra],
            out_specs=pl.BlockSpec(out, lambda n, order: (0, 0)),
            scratch_shapes=[pltpu.VMEM((2 * pairs, padded), BF16), pltpu.VMEM((pairs, rows), F32)],
        ),
        out_shape=jax.ShapeDtypeStruct(out, F32),
        name=f"contract_{count}_{len(extra)}",
    )(order, *values, high, low, *extra)


def finish_kernel(slot_ref, first_ref, second_ref, virtual_ref, parts_ref, out_ref, sums):
    pairs, rows = out_ref.shape
    per = rows // LANES
    total = parts_ref[0]
    for n in range(1, parts_ref.shape[0]):
        total += parts_ref[n]
    for a in range(pairs):
        sums[a] = total[a * per : (a + 1) * per]
    virtual = virtual_ref[...]
    for a in range(pairs):
        denominator = virtual - first_ref[a] - second_ref[a]
        value = sums[slot_ref[a]] / denominator
        for n in range(per):
            out_ref[a : a + 1, n * LANES : (n + 1) * LANES] = value[n : n + 1]


def finish(slot, first, second, virtual, parts):
    pairs = slot.shape[0]
    per = virtual.shape[0]
    smem = pl.BlockSpec(memory_space=pltpu.SMEM)
    vmem = pl.BlockSpec(memory_space=pltpu.VMEM)
    return pl.pallas_call(
        finish_kernel,
        in_specs=[smem, smem, smem, vmem, vmem],
        out_specs=vmem,
        out_shape=jax.ShapeDtypeStruct((pairs, per * LANES), F32),
        scratch_shapes=[pltpu.VMEM((pairs, per, LANES), F32)],
        name="finish",
    )(slot, first, second, virtual, parts)


def take(table, index):
    return table.at[index].get(mode="promise_in_bounds")


def body(amplitudes, singles, pair_list, mirror, slab_rows, occ_energy, vir_energy, integrals):
    owners = lax.axis_size("mem")
    groups = lax.axis_size("grp")
    member = lax.axis_index("mem")
    group = lax.axis_index("grp")
    pair_dev, _, _, width = amplitudes.shape
    pair_total = pair_dev * owners
    half = pair_total // 2
    rows = integrals.shape[0]
    chunks = -(-width // LANES)
    padded = chunks * LANES

    packed = pack(amplitudes, chunks)
    blocks = lax.all_to_all(packed, "mem", 0, 0).reshape(pair_total, chunks, LANES)

    ordered = jnp.concatenate([pair_list[:half], take(pair_list, mirror[:half])], axis=0)
    first = take(singles, ordered[:, 0])
    second = take(singles, ordered[:, 1])
    ints = jnp.transpose(integrals[:, :, 0, :], (1, 2, 0))
    from_singles, high, low = early(member.reshape(1), first, second, ints, padded)

    own_pairs = lax.dynamic_slice_in_dim(pair_list, member * pair_dev, pair_dev, 0)
    own_mirror = lax.dynamic_slice_in_dim(mirror, member * pair_dev, pair_dev, 0)
    slot = jnp.where(member < owners // 2, jnp.arange(pair_dev, dtype=jnp.int32), own_mirror % pair_dev)
    virtual = take(vir_energy, slab_rows[:, 0]) + take(vir_energy, slab_rows[:, 1])
    virtual = virtual.reshape(rows // LANES, LANES)
    first_occ, second_occ = take(occ_energy, own_pairs[:, 0]), take(occ_energy, own_pairs[:, 1])
    blocks, from_singles, high, low, slot, virtual, first_occ, second_occ = lax.optimization_barrier(
        (blocks, from_singles, high, low, slot, virtual, first_occ, second_occ)
    )

    unpacked = unpack(mirror, blocks)
    swap = lambda v, k: lax.ppermute(v, "grp", [(i, i ^ k) for i in range(groups)])
    other_chip = swap(unpacked, 2)
    other_core = swap(unpacked, 1)
    across = swap(other_chip, 1)
    total = contract(jnp.stack([group, group ^ 1]), [unpacked, other_core], high, low)
    total = contract((group ^ 2).reshape(1), [other_chip], high, low, total)
    parts = contract((group ^ 3).reshape(1), [across], high, low, total, from_singles)
    parts = lax.all_to_all(parts.reshape(owners, -1, LANES), "mem", 0, 0)
    return finish(slot, first_occ, second_occ, virtual, parts)


def solution(mesh):
    in_specs = (
        P("mem", "grp", None, None),
        P(),
        P(),
        P(),
        P("grp", None),
        P(),
        P(),
        P("grp", None, "mem", None),
    )
    out_specs = P("mem", "grp")
    return jax.shard_map(body, mesh=mesh, in_specs=in_specs, out_specs=out_specs, check_vma=False)
```

time: 455 us -> 113 us (0.25)
  the two profiles are of different devices: /device:TPU:120 before, /device:TPU:0 now
where the time goes in v1:
time: 113 us
  Pallas kernels  40.2 us (36%)
  blocking collectives  22 us (19%)
  waiting for transfers between devices  18.5 us (16%)
  local copies, waits for them, and re-layouts  17.9 us (16%)
  starting transfers between devices  11.8 us (10%)
  other arithmetic  2.08 us (2%)
    all_to_all x1, blocking collectives, body(): parts = lax.all_to_all(parts.reshape(owners, -1, LANES), 'mem', 0, 0)  22 us
    ppermute x3, waiting for transfers between devices, body(): lax.ppermute(v, 'grp', [(i, i ^ k) for i in range(groups)])  18.5 us
    pallas_call x1, Pallas kernels, early(): pl.pallas_call(early_kernel, grid=(quarters,), in_specs=[pl.BlockSpec(mem...  16.2 us
    pallas_call x3, Pallas kernels, contract(): pl.pallas_call(functools.partial(contract_kernel, count=count, has_sum=to...  15 us
    gather x8, local copies, waits for them, and re-layouts, take(): return table.at[index].get(mode='promise_in_bounds')  13.9 us
    all_to_all x1, starting transfers between devices, body(): lax.all_to_all(packed, 'mem', 0, 0).reshape(pair_total, chunks, LANES)  11.2 us
    pallas_call x1, Pallas kernels, pack(): pl.pallas_call(functools.partial(pack_kernel, chunks=chunks), grid=(pairs...  4.78 us
    unnamed x18, local copies, waits for them, and re-layouts  3.85 us
  transfers between devices with their start and end apart: 4, of which 1 were waited for; matrix products, arithmetic and copies ran while one was open for 16% of the time, Pallas kernels for 24%

profile of v1, /device:TPU:0, one launch (start us, length us, event | category | flops | bytes accessed | tf_op | source)
XLA Modules:
  0.0 112.6 jit_solution(17132264026437410235)
XLA Ops:
  0.0 0.0 copy-start
  0.0 4.8 %pack.1 = f32[32,96,128]{2,1,0:T(8,128)} custom-call(f32[6,1,32,2000]{3,2,1,0:T(8,128)} %stored_ref.1), custom_call_target="tpu_custom_call" | custom-call | tf_op jit(solution)/shard_map/pack/pallas_call | solution.py:34
  4.8 0.0 copy-start.5
  4.8 0.0 copy-start.1
  4.8 11.2 %all-to-all-start = ((f32[32,96,128]{2,1,0:T(8,128)}), f32[32,96,128]{2,1,0:T(8,128)}, u32[]{:S(2)}, u32[]{:S(2)}) async-start(f32[32,96,128]{2,1,0:T(8,128)} %pack.1), calls=%async_computation | async-start | bytes 3145728 | tf_op jit(solution)/shard_map/all_to_all | solution.py:258
  16.0 0.0 copy-done.5
  16.0 0.1 copy.17
  16.1 0.1 constant_dynamic-slice_fusion
  16.2 0.0 copy-done.1
  16.2 1.2 %gather_fusion.5 = f32[6]{0:T(128)} fusion(f32[250]{0:T(256)S(1)} %copy-done.1, s32[1024]{0:T(1024)S(1)} %get-tuple-element.34), kind=kCustom, calls=%fused_computation.5 | custom fusion | bytes 72 | tf_op jit(solution)/shard_map/gather | solution.py:242
  17.4 1.1 gather_fusion.6
  18.5 0.0 copy-start.7
  18.5 0.0 slice-start
  18.5 1.9 %copy.19 = f32[250,2000]{1,0:T(8,128)S(1)} copy(f32[250,2000]{0,1:T(8,128)} %param.9) | data formatting | bytes 4000000 | tf_op args[1]
  20.4 0.0 copy-done.7
  20.5 0.6 gather_fusion
  21.1 0.1 copy.18
  21.1 0.0 slice-done
  21.1 0.1 compare_select_fusion.2
  21.2 2.3 %gather_fusion.1 = f32[192,2000]{1,0:T(8,128)} fusion(f32[250,2000]{1,0:T(8,128)S(1)} %copy.19, s32[1024]{0:T(1024)S(1)} %pad_clamp_fusion.5), kind=kCustom, calls=%fused_computation.1 | custom fusion | bytes 3072768 | tf_op jit(solution)/shard_map/gather | solution.py:242
  23.6 0.0 copy-start.6
  23.6 2.4 %gather_fusion.2 = f32[192,2000]{1,0:T(8,128)} fusion(f32[250,2000]{1,0:T(8,128)S(1)} %copy.19, s32[1024]{0:T(1024)S(1)} %pad_clamp_fusion.4), kind=kCustom, calls=%fused_computation.2 | custom fusion | bytes 3072768 | tf_op jit(solution)/shard_map/gather | solution.py:242
  25.9 0.0 copy-done.6
  26.0 0.0 copy-done
  26.0 3.1 %gather_fusion.3 = f32[512]{0:T(512)S(1)} fusion(f32[2000]{0:T(1024)S(1)} %copy-done, s32[1024]{0:T(1024)S(1)} %pad_clamp_fusion.3), kind=kCustom, calls=%fused_computation.3 | custom fusion | bytes 6144 | tf_op jit(solution)/shard_map/gather | solution.py:242
  29.1 3.1 %gather_fusion.4 = f32[512]{0:T(512)S(1)} fusion(f32[2000]{0:T(1024)S(1)} %copy-done, s32[1024]{0:T(1024)S(1)} %pad_clamp_fusion.2), kind=kCustom, calls=%fused_computation.4 | custom fusion | bytes 6144 | tf_op jit(solution)/shard_map/gather | solution.py:242
  32.3 16.2 %early.1 = (f32[192,512]{1,0:T(8,128)}, bf16[4,2048,512]{2,1,0:T(8,128)(2,1)}, bf16[4,2048,512]{2,1,0:T(8,128)(2,1)}) custom-call(s32[1]{0:T(128)} %bitcast.1.member_ref, f32[192,2000]{1,0:T(8,128)} %gather_fusion.1, f32[192,2000]{1,0:T(8,128)} %gather_fusion.2, f32[4,2000,512]{2,1,0:T(8,128)} %bitcast.20), custom_call_target="tpu_custom_call" | custom-call | tf_op jit(solution)/shard_map/early/pallas_call | solution.py:107
  48.5 0.6 broadcast_select_fusion.slot_ref
  49.1 0.6 add_bitcast_fusion.virtual_ref
  49.7 0.0 all-to-all-done
  49.7 2.5 %unpack.1.refs_0_ = f32[96,16,128]{2,1,0:T(8,128)} custom-call(s32[192]{0:T(256)} %mirror_ref.1, f32[192,16,128]{2,1,0:T(8,128)} %bitcast.blocks_ref), custom_call_target="tpu_custom_call" | custom-call | tf_op jit(solution)/shard_map/unpack/pallas_call | solution.py:54
  52.2 0.7 collective-permute-start
  52.9 0.0 collective-permute-start.2
  52.9 18.5 %collective-permute-done.refs_0_ = f32[96,16,128]{2,1,0:T(8,128)S(1)} collective-permute-done((f32[96,16,128]{2,1,0:T(8,128)}, f32[96,16,128]{2,1,0:T(8,128)S(1)}, u32[]{:S(2)}, u32[]{:S(2)}) %collective-permute-start) | collective-permute-done | bytes 786464 | tf_op jit(solution)/shard_map/ppermute | solution.py:277
  71.4 0.0 copy-start.2
  71.4 0.0 collective-permute-start.1
  71.4 0.7 pad_add_fusion.1.order_ref
  72.1 0.0 collective-permute-done.2.refs_1_
  72.1 0.0 copy-start.4
  72.1 0.9 copy-done.4
  73.1 6.5 %contract_2_0.1.refs_3_ = f32[96,512]{1,0:T(8,128)} custom-call(s32[2]{0:T(128)} %pad_add_fusion.1.order_ref, f32[96,16,128]{2,1,0:T(8,128)} %unpack.1.refs_0_, f32[96,16,128]{2,1,0:T(8,128)} %copy-done.4, bf16[4,2048,512]{2,1,0:T(8,128)(2,1)} %get-tuple-element.24.refs_2_.refs_1_, bf16[4,2048,512]{2,1,0:T(8,128)(2,1)} %get-tuple-element.25.refs_3_.refs_2_), custom_call_target="tpu_custom_call" | custom-call | tf_op jit(solution)/shard_map/contract_2_0/pallas_call | solution.py:196
  79.6 0.0 copy-done.2
  79.6 4.2 %contract_1_1.1.refs_3_ = f32[96,512]{1,0:T(8,128)} custom-call(s32[1]{0:T(128)} %bitcast.12.order_ref, f32[96,16,128]{2,1,0:T(8,128)} %copy-done.2, bf16[4,2048,512]{2,1,0:T(8,128)(2,1)} %get-tuple-element.24.refs_2_.refs_1_, bf16[4,2048,512]{2,1,0:T(8,128)(2,1)} %get-tuple-element.25.refs_3_.refs_2_, f32[96,512]{1,0:T(8,128)} %contract_2_0.1.refs_3_), custom_call_target="tpu_custom_call" | custom-call | tf_op jit(solution)/shard_map/contract_1_1/pallas_call | solution.py:196
  83.7 0.0 collective-permute-done.1.refs_0_
  83.7 0.0 copy-start.3
  83.7 0.9 copy-done.3
  84.6 4.3 %contract_1_2.1 = f32[768,128]{1,0:T(8,128)} custom-call(s32[1]{0:T(128)} %bitcast.11.order_ref, f32[96,16,128]{2,1,0:T(8,128)} %copy-done.3, bf16[4,2048,512]{2,1,0:T(8,128)(2,1)} %get-tuple-element.24.refs_2_.refs_1_, bf16[4,2048,512]{2,1,0:T(8,128)(2,1)} %get-tuple-element.25.refs_3_.refs_2_, f32[96,512]{1,0:T(8,128)} %contract_1_1.1.refs_3_, ...), custom_call_target="tpu_custom_call" | custom-call | tf_op jit(solution)/shard_map/contract_1_2/pallas_call | solution.py:196
  89.0 22.0 %all_to_all.10.parts_ref = f32[32,24,128]{2,1,0:T(8,128)} all-to-all(f32[32,24,128]{2,1,0:T(8,128)} %bitcast.21), channel_id=1, replica_groups=mesh['grp'=4,'mem'=32] {'mem'}, dimensions={0} | all-to-all | bytes 786432 | tf_op jit(solution)/shard_map/all_to_all | solution.py:284
  111.0 1.7 %finish.1 = f32[6,512]{1,0:T(8,128)} custom-call(s32[6]{0:T(128)} %broadcast_select_fusion.slot_ref, f32[6]{0:T(128)} %gather_fusion.5, f32[6]{0:T(128)} %gather_fusion.6, f32[4,128]{1,0:T(4,128)} %add_bitcast_fusion.virtual_ref, f32[32,24,128]{2,1,0:T(8,128)} %all_to_all.10.parts_ref), custom_call_target="tpu_custom_call" | custom-call | tf_op jit(solution)/shard_map/finish/pallas_call | solution.py:231
  (9 shorter events, 0.1 us)
Async XLA Ops:
  0.0 26.0 %copy-start = (f32[2000]{0:T(1024)S(1)}, f32[2000]{0:T(1024)}, u32[]{:S(2)}) copy-start(f32[2000]{0:T(1024)} %param.14) | copy-start | bytes 24004
  4.8 11.2 %copy-start.5 = (s32[192,2]{0,1:T(2,128)S(1)}, s32[192,2]{0,1:T(2,128)}, u32[]{:S(2)}) copy-start(s32[192,2]{0,1:T(2,128)} %param.10) | copy-start | bytes 4612
  4.8 11.4 %copy-start.1 = (f32[250]{0:T(256)S(1)}, f32[250]{0:T(256)}, u32[]{:S(2)}) copy-start(f32[250]{0:T(256)} %param.13) | copy-start | bytes 3004
  4.8 44.9 %all-to-all-start = ((f32[32,96,128]{2,1,0:T(8,128)}), f32[32,96,128]{2,1,0:T(8,128)}, u32[]{:S(2)}, u32[]{:S(2)}) async-start(f32[32,96,128]{2,1,0:T(8,128)} %pack.1), calls=%async_computation | async-start | bytes 3145728 | tf_op jit(solution)/shard_map/all_to_all | solution.py:258
  18.5 1.9 %copy-start.7 = (s32[192]{0:T(256)S(1)}, s32[192]{0:T(256)}, u32[]{:S(2)}) copy-start(s32[192]{0:T(256)} %mirror_ref.1) | copy-start | bytes 2308
  18.5 2.7 %slice-start = ((s32[192,2]{0,1:T(2,128)}), s32[96,2]{0,1:T(2,128)S(1)}, s32[]{:S(2)}) async-start(s32[192,2]{0,1:T(2,128)} %param.10), calls=%async_computation.2 | async-start | bytes 2048 | tf_op jit(solution)/shard_map/slice | solution.py:260
  23.6 2.4 %copy-start.6 = (s32[512,2]{0,1:T(2,128)S(1)}, s32[512,2]{0,1:T(2,128)}, u32[]{:S(2)}) copy-start(s32[512,2]{0,1:T(2,128)} %param.12) | copy-start | bytes 12292
  52.2 19.2 %collective-permute-start = (f32[96,16,128]{2,1,0:T(8,128)}, f32[96,16,128]{2,1,0:T(8,128)S(1)}, u32[]{:S(2)}, u32[]{:S(2)}) collective-permute-start(f32[96,16,128]{2,1,0:T(8,128)} %unpack.1.refs_0_), channel_id=1, source_target_pairs={{0,64},{32,96},{64,0},{96,32},{1,65},{33,97},{65,1},{97,33},{2,66}... | collective-permute-start | bytes 2359304 | tf_op jit(solution)/shard_map/ppermute | solution.py:277
  52.9 19.3 %collective-permute-start.2 = (f32[96,16,128]{2,1,0:T(8,128)}, f32[96,16,128]{2,1,0:T(8,128)S(1)}, u32[]{:S(2)}, u32[]{:S(2)}) collective-permute-start(f32[96,16,128]{2,1,0:T(8,128)} %unpack.1.refs_0_), channel_id=1, source_target_pairs={{0,32},{32,0},{64,96},{96,64},{1,33},{33,1},{65,97},{97,65},{2,34}... | collective-permute-start | bytes 2359304 | tf_op jit(solution)/shard_map/ppermute | solution.py:277
  71.4 8.2 %copy-start.2 = (f32[96,16,128]{2,1,0:T(8,128)}, f32[96,16,128]{2,1,0:T(8,128)S(1)}, u32[]{:S(2)}) copy-start(f32[96,16,128]{2,1,0:T(8,128)S(1)} %collective-permute-done.refs_0_) | copy-start | bytes 2359300
  71.4 12.3 %collective-permute-start.1 = (f32[96,16,128]{2,1,0:T(8,128)S(1)}, f32[96,16,128]{2,1,0:T(8,128)S(1)}, u32[]{:S(2)}, u32[]{:S(2)}) collective-permute-start(f32[96,16,128]{2,1,0:T(8,128)S(1)} %collective-permute-done.refs_0_), channel_id=1, source_target_pairs={{0,32},{32,0},{64,96},{96,64},{1,33},{33,1},{65,97},{97,65},{2,34}... | collective-permute-start | bytes 2359304 | tf_op jit(solution)/shard_map/ppermute | solution.py:277
  72.1 0.9 copy-start.4
  83.7 0.9 copy-start.3

commit v2 on v0

v2 whole, which is shorter than its diff:
```python
import functools

import jax
import jax.numpy as jnp
from jax import lax
from jax.experimental import pallas as pl
from jax.experimental.pallas import tpu as pltpu
from jax.sharding import PartitionSpec as P

LANES = 128
BF16 = jnp.bfloat16
F32 = jnp.float32
X, Y_HI, Z = 4, 2, 4
CORES = 2

VMEM_SPEC = pl.BlockSpec(memory_space=pltpu.VMEM)
SMEM_SPEC = pl.BlockSpec(memory_space=pltpu.SMEM)
HBM_SPEC = pl.BlockSpec(memory_space=pltpu.HBM)


def vmem(array):
    return pltpu.with_memory_space_constraint(array, pltpu.VMEM)


def hbm(array):
    return pltpu.with_memory_space_constraint(array, pltpu.HBM)


def params(mebibytes):
    return pltpu.CompilerParams(vmem_limit_bytes=mebibytes << 20)


def split(value):
    high = value.astype(BF16)
    return high, (value - high.astype(F32)).astype(BF16)


def product(lhs, high, low):
    pairs = lhs.shape[0] // 2
    both = jnp.dot(lhs[...], high, preferred_element_type=F32)
    return both[:pairs] + both[pairs:] + jnp.dot(lhs[:pairs], low, preferred_element_type=F32)


def split_rows(values, high_ref, low_ref):
    width, rows = values.shape
    high, low = split(values)
    high_ref[:width] = high
    low_ref[:width] = low
    tail = jnp.zeros((high_ref.shape[0] - width, rows), BF16)
    high_ref[width:] = tail
    low_ref[width:] = tail


def pack_kernel(stored_ref, packed_ref, *, chunks):
    pair = pl.program_id(0)
    width = stored_ref.shape[3]
    for x in range(X):
        tile = stored_ref[0, 0, x * Y_HI * Z : (x + 1) * Y_HI * Z, :]
        tile = jnp.concatenate([tile, jnp.zeros((Y_HI * Z, chunks * LANES - width), F32)], axis=1)
        tile = tile.reshape(Y_HI * Z, chunks, LANES)
        at = pl.ds(pl.multiple_of(pair * chunks, chunks), chunks)
        for y in range(Y_HI):
            packed_ref[x * Z : (x + 1) * Z, y, at, :] = tile[y * Z : (y + 1) * Z]


def pack(stored, chunks):
    pairs, _, offsets, width = stored.shape
    return pl.pallas_call(
        functools.partial(pack_kernel, chunks=chunks),
        grid=(pairs,),
        in_specs=[pl.BlockSpec((1, 1, offsets, width), lambda p: (p, 0, 0, 0))],
        out_specs=VMEM_SPEC,
        out_shape=pltpu.VMEM((X * Z, Y_HI, pairs * chunks, LANES), F32),
        compiler_params=params(8),
        name="pack",
    )(stored)


def unpack_kernel(place_ref, mirror_ref, lower_ref, upper_ref, out_ref, *, sources):
    step = pl.program_id(0)
    pairs = lower_ref.shape[2]
    for n in range(sources):
        source = step * sources + n
        owner = source // Z * (Y_HI * Z) + place_ref[0] * Z + source % Z
        for a in range(pairs):
            slot = lax.rem(mirror_ref[owner * pairs + a], pairs)
            out_ref[:, source * pairs + a, :] = lower_ref[n, 0, a] - upper_ref[n, 0, slot]


def unpack(place, mirror, blocks):
    count, _, pairs, chunks, lanes = blocks.shape
    half, steps = count // 2, 2
    side = lambda shift: pl.BlockSpec(
        (half // steps, 1, pairs, chunks, lanes), lambda n, place, mirror: (n + shift, place[1], 0, 0, 0)
    )
    return pl.pallas_call(
        functools.partial(unpack_kernel, sources=half // steps),
        grid_spec=pltpu.PrefetchScalarGridSpec(
            num_scalar_prefetch=2,
            grid=(steps,),
            in_specs=[side(0), side(steps)],
            out_specs=VMEM_SPEC,
        ),
        out_shape=pltpu.VMEM((chunks, half * pairs, lanes), F32),
        compiler_params=params(8),
    )(place, mirror, blocks, blocks)


def exact(chosen, table, contract):
    total = None
    for _ in range(3):
        piece = table.astype(BF16)
        table = table - piece.astype(F32)
        part = lax.dot_general(chosen, piece, (contract, ((), ())), preferred_element_type=F32)
        total = part if total is None else total + part
    return total


def quarter(q, rows, member, lhs, ints, high_ref, low_ref, copy):
    _, pairs, width = rows.shape
    chosen = lax.broadcasted_iota(jnp.int32, (pairs, LANES), 1) == q * (X * Y_HI * Z) + member
    first_c = jnp.sum(jnp.where(chosen, rows[0, :, :LANES], 0.0), axis=1, keepdims=True)
    second_c = jnp.sum(jnp.where(chosen, rows[1, :, :LANES], 0.0), axis=1, keepdims=True)
    for start in range(0, width, LANES):
        at = slice(start, min(start + LANES, width))
        part = first_c * rows[1, :, at] - second_c * rows[0, :, at]
        part_high, part_low = split(part)
        lhs[:pairs, at] = part_high
        lhs[pairs:, at] = part_low
    copy.wait()
    split_rows(ints[...], high_ref, low_ref)
    return product(lhs, high_ref[...], low_ref[...])


def clear(lhs, width):
    full = width // LANES * LANES
    lhs[:, full:] = jnp.zeros((lhs.shape[0], lhs.shape[1] - full), BF16)


def early_kernel(
    member_ref, pairs_ref, singles_ref, ints_ref, sum_ref, high_out, low_out,
    ints, sems, rows, lhs, high, low, out_sems,
):
    count, width, _ = ints.shape
    copies = [pltpu.make_async_copy(ints_ref.at[q], ints.at[q], sems.at[q]) for q in range(count)]
    for copy in copies:
        copy.start()
    pairs, orbitals = pairs_ref.shape[0], singles_ref.shape[1]
    clear(lhs, width)
    orbital = lax.broadcasted_iota(jnp.int32, (pairs, orbitals), 1)
    for side in range(2):
        chosen = (orbital == pairs_ref[:, side : side + 1]).astype(F32).astype(BF16)
        rows[side] = exact(chosen, singles_ref[...], ((1,), (1,)))
    total = None
    outs = []
    for q in range(count):
        slot = q % 2
        for out in outs[2 * (q - 2) : 2 * (q - 1)] if q > 1 else []:
            out.wait()
        part = quarter(q, rows, member_ref[0], lhs, ints.at[q], high.at[slot], low.at[slot], copies[q])
        total = part if total is None else total + part
        for n, (here, there) in enumerate(((high, high_out), (low, low_out))):
            outs.append(pltpu.make_async_copy(here.at[slot], there.at[q], out_sems.at[n, q]))
            outs[-1].start()
    sum_ref[...] = total
    for out in outs[-4:]:
        out.wait()


def early(member, pairs, singles, ints, padded):
    count = pairs.shape[0]
    quarters, width, rows = ints.shape
    return pl.pallas_call(
        early_kernel,
        in_specs=[SMEM_SPEC] + [VMEM_SPEC] * 2 + [HBM_SPEC],
        out_specs=[VMEM_SPEC] + [HBM_SPEC] * 2,
        out_shape=[jax.ShapeDtypeStruct((count, rows), F32)] + [pltpu.HBM((quarters, padded, rows), BF16)] * 2,
        scratch_shapes=[
            pltpu.VMEM((quarters, width, rows), F32),
            pltpu.SemaphoreType.DMA((quarters,)),
            pltpu.VMEM((2, count, width), F32),
            pltpu.VMEM((2 * count, padded), BF16),
            pltpu.VMEM((2, padded, rows), BF16),
            pltpu.VMEM((2, padded, rows), BF16),
            pltpu.SemaphoreType.DMA((2, quarters)),
        ],
        compiler_params=params(48),
        name="early",
    )(member, pairs, singles, ints)


def virtual_kernel(slab_ref, energies_ref, out_ref):
    rows = slab_ref.shape[1]
    coarse = lax.broadcasted_iota(jnp.int32, (energies_ref.shape[1], rows), 0)
    fine = lax.broadcasted_iota(jnp.int32, (LANES, rows), 0)
    total = None
    for side in range(2):
        orbital = slab_ref[side : side + 1, :]
        chosen = (coarse == orbital // LANES).astype(F32).astype(BF16)
        rest, columns = energies_ref[...], None
        for _ in range(3):
            piece = rest.astype(BF16)
            rest = rest - piece.astype(F32)
            part = jnp.dot(piece, chosen, preferred_element_type=F32)
            columns = part if columns is None else columns + part
        energy = jnp.sum(jnp.where(fine == orbital % LANES, columns, 0.0), axis=0, keepdims=True)
        total = energy if total is None else total + energy
    for n in range(rows // LANES):
        out_ref[n : n + 1, :] = total[:, n * LANES : (n + 1) * LANES]


def virtual_sums(slab, energies):
    return pl.pallas_call(
        virtual_kernel,
        in_specs=[VMEM_SPEC] * 2,
        out_specs=VMEM_SPEC,
        out_shape=jax.ShapeDtypeStruct((slab.shape[1] // LANES, LANES), F32),
        compiler_params=params(8),
        name="virtual",
    )(slab, energies)


def fill(lhs, values):
    half = lhs.shape[0] // 2
    row = 0
    for value_ref in values:
        chunks, pairs, _ = value_ref.shape
        for k in range(chunks):
            high, low = split(value_ref[k])
            at = slice(k * LANES, (k + 1) * LANES)
            lhs[row : row + pairs, at] = high
            lhs[half + row : half + row + pairs, at] = low
        row += pairs


def own_kernel(place_ref, value_ref, high_in, low_in, high_ref, low_ref, out_ref, sems, lhs):
    quarters = high_ref.shape[0]
    order = [place_ref[2] ^ n for n in range(quarters)]
    copies = [
        pltpu.make_async_copy(there.at[q], here.at[q], sems.at[n, m])
        for m, q in enumerate(order)
        for n, (there, here) in enumerate(((high_in, high_ref), (low_in, low_ref)))
    ]
    for copy in copies:
        copy.start()
    fill(lhs, [value_ref])
    copies[0].wait()
    copies[1].wait()
    pairs = value_ref.shape[1]
    out_ref[:pairs] = product(lhs, high_ref[order[0]], low_ref[order[0]])
    out_ref[pairs:] = jnp.zeros_like(out_ref[pairs:])
    for copy in copies[2:]:
        copy.wait()


def own(place, value, high, low):
    _, pairs, _ = value.shape
    quarters, padded, rows = high.shape
    return pl.pallas_call(
        own_kernel,
        in_specs=[SMEM_SPEC, VMEM_SPEC, HBM_SPEC, HBM_SPEC],
        out_specs=[VMEM_SPEC] * 3,
        out_shape=[
            pltpu.VMEM(high.shape, BF16),
            pltpu.VMEM(low.shape, BF16),
            pltpu.VMEM((2 * pairs, rows), F32),
        ],
        scratch_shapes=[pltpu.SemaphoreType.DMA((2, quarters)), pltpu.VMEM((2 * pairs, padded), BF16)],
        compiler_params=params(8),
        name="own",
    )(place, vmem(value), hbm(high), hbm(low))


def contract_kernel(place_ref, *refs, flip, first, count, fresh, last):
    values, (high_ref, low_ref, *rest) = refs[:count], refs[count:]
    if not fresh:
        sum_ref, *rest = rest
    if last:
        singles_ref, *rest = rest
    out_ref, lhs = rest
    pairs = lhs.shape[0] // 2
    fill(lhs, values)
    quarter = place_ref[2] ^ flip
    part = product(lhs, high_ref[quarter], low_ref[quarter])
    if not last:
        for row in range(0, out_ref.shape[0], pairs):
            at = slice(row, row + pairs)
            if fresh:
                out_ref[at] = part if row == first else jnp.zeros_like(part)
            else:
                out_ref[at] = sum_ref[at] + part if row == first else sum_ref[at]
        return
    total = [sum_ref[row : row + pairs] + (part if row == first else 0.0) for row in (0, pairs)]
    per = part.shape[1] // LANES
    group = pairs // 2
    sides = singles_ref.shape[0] // 2
    for y, sums in enumerate(total):
        place = place_ref[y]
        for x in range(2):
            for mirrored in range(2):
                row = mirrored * sides + x * Y_HI * group + place * group
                mine = singles_ref[pl.ds(pl.multiple_of(row, 8), group), :]
                ours = sums[x * group : (x + 1) * group]
                full = 0.5 * (mine - ours if mirrored else mine + ours)
                for a in range(0, group, 8):
                    for n in range(per):
                        at = pl.ds((row + a) * per + n, 8, stride=per)
                        out_ref[at, :] = full[a : a + 8, n * LANES : (n + 1) * LANES]


def contract(place, flip, values, first, high, low, total=None, singles=None):
    count = len(values)
    _, pairs, _ = values[0].shape
    _, padded, rows = high.shape
    last = singles is not None
    inputs = [*values, high, low] + [a for a in (total, singles) if a is not None]
    out = (4 * pairs * rows // LANES, LANES) if last else (2 * pairs, rows)
    return pl.pallas_call(
        functools.partial(
            contract_kernel, flip=flip, first=first, count=count, fresh=total is None, last=last
        ),
        in_specs=[SMEM_SPEC] + [VMEM_SPEC] * len(inputs),
        out_specs=VMEM_SPEC,
        out_shape=pltpu.VMEM(out, F32),
        scratch_shapes=[pltpu.VMEM((2 * pairs * count, padded), BF16)],
        compiler_params=params(8),
    )(place, *(vmem(a) for a in inputs))


def finish_kernel(member_ref, mirror_ref, pairs_ref, occupied_ref, virtual_ref, parts_ref, out_ref, sums):
    pairs, rows = out_ref.shape
    per = rows // LANES
    member = member_ref[0]
    total = parts_ref[0]
    for n in range(1, parts_ref.shape[0]):
        total += parts_ref[n]
    for a in range(pairs):
        sums[a] = total[a * per : (a + 1) * per]
    for a in range(pairs):
        pair = member * pairs + a
        denominator = virtual_ref[...] - occupied_ref[pairs_ref[0, pair]] - occupied_ref[pairs_ref[1, pair]]
        slot = jnp.where(member < parts_ref.shape[0] // 2, a, lax.rem(mirror_ref[pair], pairs))
        value = sums[slot] / denominator
        for n in range(per):
            out_ref[a : a + 1, n * LANES : (n + 1) * LANES] = value[n : n + 1]


def finish(member, mirror, pairs, occupied, virtual, parts):
    _, block, _ = parts.shape
    per = virtual.shape[0]
    count = block // per
    return pl.pallas_call(
        finish_kernel,
        in_specs=[SMEM_SPEC] * 4 + [VMEM_SPEC] * 2,
        out_specs=VMEM_SPEC,
        out_shape=jax.ShapeDtypeStruct((count, per * LANES), F32),
        scratch_shapes=[pltpu.VMEM((count, per, LANES), F32)],
        compiler_params=params(8),
        name="finish",
    )(member, mirror, pairs, occupied, virtual, parts)


def neighbour(device):
    group, member = divmod(device, X * Y_HI * Z)
    y_lo, core = divmod(group, CORES)
    x, place = divmod(member, Y_HI * Z)
    y_hi, z = divmod(place, Z)
    y = y_hi * 2 + y_lo
    y = y + 1 if y % 2 else y - 1
    y_hi, y_lo = divmod(y % (2 * Y_HI), 2)
    return (y_lo * CORES + core) * (X * Y_HI * Z) + (x * Y_HI + y_hi) * Z + z


def body(amplitudes, singles, pair_list, mirror, slab_rows, occ_energy, vir_energy, integrals):
    owners = lax.axis_size("mem")
    groups = lax.axis_size("grp")
    member = lax.axis_index("mem").reshape(1)
    group = lax.axis_index("grp").reshape(1)
    pair_dev, _, _, width = amplitudes.shape
    half = pair_dev * owners // 2
    chunks = -(-width // LANES)
    padded = chunks * LANES

    def swap(value, flip):
        return lax.ppermute(value, "grp", [(i, i ^ flip) for i in range(groups)])

    planes = [[(x * Y_HI + y) * Z + z for x in range(X) for z in range(Z)] for y in range(Y_HI)]
    packed = pack(amplitudes, chunks)
    blocks = lax.all_to_all(packed, "mem", 0, 0, axis_index_groups=planes)
    blocks = blocks.reshape(X * Z, Y_HI, pair_dev, chunks, LANES)

    ordered = jnp.concatenate([pair_list[:half], pair_list.at[mirror[:half]].get(mode="promise_in_bounds")], axis=0)
    ints = hbm(jnp.transpose(integrals[:, :, 0, :], (1, 2, 0)))
    from_singles, high, low = early(member, ordered, singles.T, ints, padded)
    y_hi = member // Z % Y_HI
    place = jnp.concatenate([y_hi, 1 - y_hi, group])
    ours = jnp.concatenate([y_hi, y_hi])
    theirs = jnp.concatenate([y_hi, 1 - y_hi])
    blocks, from_singles, high, low, place, ours, theirs, member = lax.optimization_barrier(
        (blocks, from_singles, high, low, place, ours, theirs, member)
    )

    away = unpack(theirs, mirror, blocks)
    pairs = away.shape[1]
    from_near = lax.ppermute(away, ("grp", "mem"), [(i, neighbour(i)) for i in range(groups * owners)])
    home = unpack(ours, mirror, blocks)
    from_chip = swap(home, 2)
    from_core = swap(home, 1)
    high, low, total = own(place, home, high, low)
    passed = swap(from_near, 2)
    core_near = swap(from_near, 1)
    core_chip = swap(from_chip, 1)
    total = contract(place, 1, [from_core], 0, high, low, total)
    total = contract(place, 2, [from_chip, from_near], 0, high, low, total)
    total = contract(place, 3, [core_chip, core_near], 0, high, low, total)
    passed, total = lax.optimization_barrier((passed, total))
    core_passed = swap(passed, 1)
    total = contract(place, 0, [passed], pairs, high, low, total)
    total = contract(place, 1, [core_passed], pairs, high, low, total, from_singles)

    total, vir_energy, slab_rows = lax.optimization_barrier((total, vir_energy, slab_rows))
    parts = lax.all_to_all(total.reshape(owners, -1, LANES), "mem", 0, 0)
    energies = jnp.pad(vir_energy, (0, padded - width)).reshape(chunks, LANES).T
    virtual = virtual_sums(slab_rows.T, energies)
    return finish(member, mirror, pair_list.T, occ_energy, virtual, parts)


def solution(mesh):
    in_specs = (
        P("mem", "grp", None, None),
        P(),
        P(),
        P(),
        P("grp", None),
        P(),
        P(),
        P("grp", None, "mem", None),
    )
    out_specs = P("mem", "grp")

    return jax.shard_map(body, mesh=mesh, in_specs=in_specs, out_specs=out_specs, check_vma=False)
```

time: 455 us -> 84.6 us (0.19)
  the two profiles are of different devices: /device:TPU:120 before, /device:TPU:0 now
where the time goes in v2:
time: 84.6 us; the launch traced here: 84.2 us
  Pallas kernels  33.8 us (40%)
  waiting for transfers between devices  24.3 us (29%)
  starting transfers between devices  19.7 us (23%)
  local copies, waits for them, and re-layouts  5.31 us (6%)
  other arithmetic  0.85 us (1%)
    pallas_call x1, Pallas kernels, early(): pl.pallas_call(early_kernel, in_specs=[SMEM_SPEC] + [VMEM_SPEC] * 2 + [HB...  14.4 us
    all_to_all x1, waiting for transfers between devices, body(): parts = lax.all_to_all(total.reshape(owners, -1, LANES), 'mem', 0, 0)  11.8 us
    all_to_all x1, starting transfers between devices, body(): blocks = lax.all_to_all(packed, 'mem', 0, 0, axis_index_groups=planes)  7.99 us
    pallas_call x5, Pallas kernels, contract(): pl.pallas_call(functools.partial(contract_kernel, flip=flip, first=first,...  7.83 us
    all_to_all x1, starting transfers between devices, body(): parts = lax.all_to_all(total.reshape(owners, -1, LANES), 'mem', 0, 0)  7.83 us
    pallas_call x1, Pallas kernels, own(): pl.pallas_call(own_kernel, in_specs=[SMEM_SPEC, VMEM_SPEC, HBM_SPEC, HBM_...  6.47 us
    all_to_all x1, waiting for transfers between devices, body(): blocks = lax.all_to_all(packed, 'mem', 0, 0, axis_index_groups=planes)  4.72 us
    ppermute x6, waiting for transfers between devices, swap(): return lax.ppermute(value, 'grp', [(i, i ^ flip) for i in range(groups)])  3.9 us
  transfers between devices with their start and end apart: 9, of which 6 were waited for; matrix products, arithmetic and copies ran while one was open for 4% of the time, Pallas kernels for 33%

profile of v2, /device:TPU:0, one launch (start us, length us, event | category | flops | bytes accessed | tf_op | source)
XLA Modules:
  0.0 84.2 jit_solution(4941680708435095479)
XLA Ops:
  0.0 0.0 copy-start.1
  0.0 1.4 %copy-done.1 = f32[6,1,32,2000]{3,2,1,0:T(8,128)S(1)} copy-done((f32[6,1,32,2000]{3,2,1,0:T(8,128)S(1)}, f32[6,1,32,2000]{3,2,1,0:T(8,128)}, u32[]{:S(2)}) %copy-start.1) | copy-done | bytes 1536024
  1.4 1.5 %pack.1 = f32[16,2,96,128]{3,2,1,0:T(8,128)} custom-call(f32[6,1,32,2000]{3,2,1,0:T(8,128)S(1)} %copy-done.1), custom_call_target="tpu_custom_call" | custom-call | tf_op jit(solution)/shard_map/pack/pallas_call | solution.py:68
  2.9 8.0 %all-to-all-start = ((f32[16,2,96,128]{3,2,1,0:T(8,128)}), f32[16,2,96,128]{3,2,1,0:T(8,128)S(1)}, u32[]{:S(2)}, u32[]{:S(2)}) async-start(f32[16,2,96,128]{3,2,1,0:T(8,128)} %pack.1), calls=%async_computation | async-start | bytes 3145728 | tf_op jit(solution)/shard_map/all_to_all | solution.py:389
  10.9 0.7 slice.6
  11.6 0.8 copy.18
  12.4 0.1 copy.19
  12.5 0.7 compare_select_fusion
  13.2 0.6 gather_fusion
  13.8 0.0 copy-start
  13.9 1.6 %copy-done = f32[250,2000]{0,1:T(8,128)S(1)} copy-done((f32[250,2000]{0,1:T(8,128)S(1)}, f32[250,2000]{0,1:T(8,128)}, u32[]{:S(2)}) %copy-start) | copy-done | bytes 2000024
  15.4 0.0 copy-start.3
  15.4 14.4 %early.1 = (f32[192,512]{1,0:T(8,128)S(1)}, bf16[4,2048,512]{2,1,0:T(8,128)(2,1)}, bf16[4,2048,512]{2,1,0:T(8,128)(2,1)}) custom-call(s32[1]{0:T(128)} %bitcast.1.member_ref, s32[192,2]{1,0:T(8,128)S(1)} %pad_add_fusion.pairs_ref, f32[2000,250]{1,0:T(8,128)S(1)} %bitcast.17, f32[4,2000,512]{2,1,0:T(8,128)} %bitcast.21), custom_call_target="tpu_custom_call" | custom-call | tf_op jit(solution)/shard_map/early/pallas_call | solution.py:173
  29.8 0.1 pad_add_fusion.1.place_ref
  29.9 0.1 pad_add_fusion.2
  30.0 4.7 %all-to-all-done = f32[16,2,96,128]{3,2,1,0:T(8,128)S(1)} async-done(((f32[16,2,96,128]{3,2,1,0:T(8,128)}), f32[16,2,96,128]{3,2,1,0:T(8,128)S(1)}, u32[]{:S(2)}, u32[]{:S(2)}) %all-to-all-start) | async-done | bytes 1572896 | tf_op jit(solution)/shard_map/all_to_all | solution.py:389
  34.7 0.0 copy-done.3
  34.7 1.0 %shard_map.83.value_ref = f32[16,48,128]{2,1,0:T(8,128)S(1)} custom-call(s32[2]{0:T(128)S(1)} %get-tuple-element.31.place_ref, s32[192]{0:T(256)S(1)} %copy-done.3, f32[16,2,6,16,128]{4,3,2,1,0:T(8,128)S(1)} %bitcast.13, f32[16,2,6,16,128]{4,3,2,1,0:T(8,128)S(1)} %bitcast.14), custom_call_target="tpu_custom_call" | custom-call | tf_op jit(solution)/shard_map/pallas_call | solution.py:96
  35.7 1.7 %collective-permute-start.2 = (f32[16,48,128]{2,1,0:T(8,128)S(1)}, f32[16,48,128]{2,1,0:T(8,128)S(1)}, u32[]{:S(2)}, u32[]{:S(2)}) collective-permute-start(f32[16,48,128]{2,1,0:T(8,128)S(1)} %shard_map.83.value_ref), channel_id=1, source_target_pairs={{0,64},{32,96},{64,0},{96,32},{1,65},{33,97},{65,1},{97,33},{2,66}... | collective-permute-start | bytes 1179656 | tf_op jit(solution)/shard_map/ppermute | solution.py:385
  37.3 1.0 %shard_map.82 = f32[16,48,128]{2,1,0:T(8,128)S(1)} custom-call(s32[2]{0:T(128)S(1)} %get-tuple-element.29.place_ref, s32[192]{0:T(256)S(1)} %copy-done.3, f32[16,2,6,16,128]{4,3,2,1,0:T(8,128)S(1)} %bitcast.15, f32[16,2,6,16,128]{4,3,2,1,0:T(8,128)S(1)} %bitcast.16), custom_call_target="tpu_custom_call" | custom-call | tf_op jit(solution)/shard_map/pallas_call | solution.py:96
  38.4 2.3 %collective-permute-start = (f32[16,48,128]{2,1,0:T(8,128)S(1)}, f32[16,48,128]{2,1,0:T(8,128)S(1)}, u32[]{:S(2)}, u32[]{:S(2)}) collective-permute-start(f32[16,48,128]{2,1,0:T(8,128)S(1)} %shard_map.82), channel_id=1, source_target_pairs={{0,68},{1,69},{2,70},{3,71},{4,64},{5,65},{6,66},{7,67},{8,76},{9,... | collective-permute-start | bytes 1179656 | tf_op jit(solution)/shard_map/ppermute | solution.py:405
  40.6 0.0 collective-permute-start.5
  40.6 2.9 %collective-permute-done.2.refs_0_ = f32[16,48,128]{2,1,0:T(8,128)S(1)} collective-permute-done((f32[16,48,128]{2,1,0:T(8,128)S(1)}, f32[16,48,128]{2,1,0:T(8,128)S(1)}, u32[]{:S(2)}, u32[]{:S(2)}) %collective-permute-start.2) | collective-permute-done | bytes 393248 | tf_op jit(solution)/shard_map/ppermute | solution.py:385
  43.5 0.0 collective-permute-start.3
  43.6 3.9 %collective-permute-done.refs_1_ = f32[16,48,128]{2,1,0:T(8,128)S(1)} collective-permute-done((f32[16,48,128]{2,1,0:T(8,128)S(1)}, f32[16,48,128]{2,1,0:T(8,128)S(1)}, u32[]{:S(2)}, u32[]{:S(2)}) %collective-permute-start) | collective-permute-done | bytes 393248 | tf_op jit(solution)/shard_map/ppermute | solution.py:405
  47.4 0.0 collective-permute-start.4
  47.4 0.0 collective-permute-start.1
  47.4 6.5 %own.1 = (bf16[4,2048,512]{2,1,0:T(8,128)(2,1)S(1)}, bf16[4,2048,512]{2,1,0:T(8,128)(2,1)S(1)}, f32[96,512]{1,0:T(8,128)S(1)}) custom-call(s32[3]{0:T(128)S(1)} %pad_add_fusion.1.place_ref, f32[16,48,128]{2,1,0:T(8,128)S(1)} %shard_map.83.value_ref, bf16[4,2048,512]{2,1,0:T(8,128)(2,1)} %get-tuple-element.32.high_in, ...), custom_call_target="tpu_custom_call" | custom-call | tf_op jit(solution)/shard_map/own/pallas_call | solution.py:259
  53.9 0.0 collective-permute-done.5.refs_0_
  53.9 1.4 %shard_map.84.refs_4_ = f32[96,512]{1,0:T(8,128)S(1)} custom-call(s32[3]{0:T(128)S(1)} %pad_add_fusion.1.place_ref, f32[16,48,128]{2,1,0:T(8,128)S(1)} %collective-permute-done.5.refs_0_, bf16[4,2048,512]{2,1,0:T(8,128)(2,1)S(1)} %get-tuple-element.34.refs_1_.refs_2_, bf16[4,2048,512]{2,1,0:T(8,128)(2,1)S(1)} %get-tuple-element.35.refs_2_.refs_3_, ...), custom_call_target="tpu_custom_call" | custom-call | tf_op jit(solution)/shard_map/pallas_call | solution.py:318
  55.3 1.5 %shard_map.85.refs_4_ = f32[96,512]{1,0:T(8,128)S(1)} custom-call(s32[3]{0:T(128)S(1)} %pad_add_fusion.1.place_ref, f32[16,48,128]{2,1,0:T(8,128)S(1)} %collective-permute-done.2.refs_0_, f32[16,48,128]{2,1,0:T(8,128)S(1)} %collective-permute-done.refs_1_, bf16[4,2048,512]{2,1,0:T(8,128)(2,1)S(1)} %get-tuple-element.34.refs_1_.refs_2_, ...), custom_call_target="tpu_custom_call" | custom-call | tf_op jit(solution)/shard_map/pallas_call | solution.py:318
  56.8 0.0 collective-permute-done.3.refs_0_
  56.8 0.0 collective-permute-done.4.refs_1_
  56.8 1.5 %shard_map.86.refs_3_ = f32[96,512]{1,0:T(8,128)S(1)} custom-call(s32[3]{0:T(128)S(1)} %pad_add_fusion.1.place_ref, f32[16,48,128]{2,1,0:T(8,128)S(1)} %collective-permute-done.3.refs_0_, f32[16,48,128]{2,1,0:T(8,128)S(1)} %collective-permute-done.4.refs_1_, bf16[4,2048,512]{2,1,0:T(8,128)(2,1)S(1)} %get-tuple-element.34.refs_1_.refs_2_, ...), custom_call_target="tpu_custom_call" | custom-call | tf_op jit(solution)/shard_map/pallas_call | solution.py:318
  58.3 0.7 collective-permute-done.1.refs_0_
  59.0 0.0 collective-permute-start.6
  59.0 1.4 %shard_map.87.refs_3_ = f32[96,512]{1,0:T(8,128)S(1)} custom-call(s32[3]{0:T(128)S(1)} %pad_add_fusion.1.place_ref, f32[16,48,128]{2,1,0:T(8,128)S(1)} %collective-permute-done.1.refs_0_, bf16[4,2048,512]{2,1,0:T(8,128)(2,1)S(1)} %get-tuple-element.34.refs_1_.refs_2_, bf16[4,2048,512]{2,1,0:T(8,128)(2,1)S(1)} %get-tuple-element.35.refs_2_.refs_3_, ...), custom_call_target="tpu_custom_call" | custom-call | tf_op jit(solution)/shard_map/pallas_call | solution.py:318
  60.3 0.0 copy-start.6
  60.3 0.0 copy-start.4
  60.4 0.0 copy-start.2
  60.4 0.0 copy-start.5
  60.4 0.3 collective-permute-done.6.refs_0_
  60.7 2.1 %shard_map.88 = f32[768,128]{1,0:T(8,128)} custom-call(s32[3]{0:T(128)S(1)} %pad_add_fusion.1.place_ref, f32[16,48,128]{2,1,0:T(8,128)S(1)} %collective-permute-done.6.refs_0_, bf16[4,2048,512]{2,1,0:T(8,128)(2,1)S(1)} %get-tuple-element.34.refs_1_.refs_2_, bf16[4,2048,512]{2,1,0:T(8,128)(2,1)S(1)} %get-tuple-element.35.refs_2_.refs_3_, ...), custom_call_target="tpu_custom_call" | custom-call | tf_op jit(solution)/shard_map/pallas_call | solution.py:318
  62.8 7.8 %all-to-all-start.1 = ((f32[32,24,128]{2,1,0:T(8,128)}), f32[32,24,128]{2,1,0:T(8,128)S(1)}, u32[]{:S(2)}, u32[]{:S(2)}) async-start(f32[32,24,128]{2,1,0:T(8,128)} %bitcast.10), calls=%async_computation.1 | async-start | bytes 786432 | tf_op jit(solution)/shard_map/all_to_all | solution.py:422
  70.6 0.0 copy-done.6
  70.7 0.1 copy.20
  70.8 0.0 copy-done.4
  70.8 0.4 virtual.1.virtual_ref
  71.1 11.8 %all-to-all-done.1.parts_ref = f32[32,24,128]{2,1,0:T(8,128)S(1)} async-done(((f32[32,24,128]{2,1,0:T(8,128)}), f32[32,24,128]{2,1,0:T(8,128)S(1)}, u32[]{:S(2)}, u32[]{:S(2)}) %all-to-all-start.1) | async-done | bytes 393248 | tf_op jit(solution)/shard_map/all_to_all | solution.py:422
  82.9 0.0 copy-done.2
  82.9 0.0 copy-done.5
  82.9 1.2 %finish.1 = f32[6,512]{1,0:T(8,128)} custom-call(s32[1]{0:T(128)} %bitcast.1.member_ref, s32[192]{0:T(256)S(1)} %copy-done.3, s32[2,192]{1,0:T(2,128)S(1)} %bitcast.19, f32[250]{0:T(256)S(1)} %copy-done.5, f32[4,128]{1,0:T(4,128)S(1)} %virtual.1.virtual_ref, f32[32,24,128]{2,1,0:T(8,128)S(1)} %all-to-all-done.1.parts_ref), custom_call_target="tpu_custom_call" | custom-call | tf_op jit(solution)/shard_map/finish/pallas_call | solution.py:352
  (3 shorter events, 0.0 us)
Async XLA Ops:
  0.0 1.4 %copy-start.1 = (f32[6,1,32,2000]{3,2,1,0:T(8,128)S(1)}, f32[6,1,32,2000]{3,2,1,0:T(8,128)}, u32[]{:S(2)}) copy-start(f32[6,1,32,2000]{3,2,1,0:T(8,128)} %stored_ref.1) | copy-start | bytes 4608004
  2.9 31.8 %all-to-all-start = ((f32[16,2,96,128]{3,2,1,0:T(8,128)}), f32[16,2,96,128]{3,2,1,0:T(8,128)S(1)}, u32[]{:S(2)}, u32[]{:S(2)}) async-start(f32[16,2,96,128]{3,2,1,0:T(8,128)} %pack.1), calls=%async_computation | async-start | bytes 3145728 | tf_op jit(solution)/shard_map/all_to_all | solution.py:389
  13.8 1.6 %copy-start = (f32[250,2000]{0,1:T(8,128)S(1)}, f32[250,2000]{0,1:T(8,128)}, u32[]{:S(2)}) copy-start(f32[250,2000]{0,1:T(8,128)} %param.9) | copy-start | bytes 6000004
  15.4 19.3 %copy-start.3 = (s32[192]{0:T(256)S(1)}, s32[192]{0:T(256)}, u32[]{:S(2)}) copy-start(s32[192]{0:T(256)} %mirror_ref.5) | copy-start | bytes 2308
  35.7 7.9 %collective-permute-start.2 = (f32[16,48,128]{2,1,0:T(8,128)S(1)}, f32[16,48,128]{2,1,0:T(8,128)S(1)}, u32[]{:S(2)}, u32[]{:S(2)}) collective-permute-start(f32[16,48,128]{2,1,0:T(8,128)S(1)} %shard_map.83.value_ref), channel_id=1, source_target_pairs={{0,64},{32,96},{64,0},{96,32},{1,65},{33,97},{65,1},{97,33},{2,66}... | collective-permute-start | bytes 1179656 | tf_op jit(solution)/shard_map/ppermute | solution.py:385
  38.4 9.1 %collective-permute-start = (f32[16,48,128]{2,1,0:T(8,128)S(1)}, f32[16,48,128]{2,1,0:T(8,128)S(1)}, u32[]{:S(2)}, u32[]{:S(2)}) collective-permute-start(f32[16,48,128]{2,1,0:T(8,128)S(1)} %shard_map.82), channel_id=1, source_target_pairs={{0,68},{1,69},{2,70},{3,71},{4,64},{5,65},{6,66},{7,67},{8,76},{9,... | collective-permute-start | bytes 1179656 | tf_op jit(solution)/shard_map/ppermute | solution.py:405
  40.6 13.3 %collective-permute-start.5 = (f32[16,48,128]{2,1,0:T(8,128)S(1)}, f32[16,48,128]{2,1,0:T(8,128)S(1)}, u32[]{:S(2)}, u32[]{:S(2)}) collective-permute-start(f32[16,48,128]{2,1,0:T(8,128)S(1)} %shard_map.83.value_ref), channel_id=1, source_target_pairs={{0,32},{32,0},{64,96},{96,64},{1,33},{33,1},{65,97},{97,65},{2,34}... | collective-permute-start | bytes 1179656 | tf_op jit(solution)/shard_map/ppermute | solution.py:385
  43.5 13.2 %collective-permute-start.3 = (f32[16,48,128]{2,1,0:T(8,128)S(1)}, f32[16,48,128]{2,1,0:T(8,128)S(1)}, u32[]{:S(2)}, u32[]{:S(2)}) collective-permute-start(f32[16,48,128]{2,1,0:T(8,128)S(1)} %collective-permute-done.2.refs_0_), channel_id=1, source_target_pairs={{0,32},{32,0},{64,96},{96,64},{1,33},{33,1},{65,97},{97,65},{2,34}... | collective-permute-start | bytes 1179656 | tf_op jit(solution)/shard_map/ppermute | solution.py:385
  47.4 9.4 %collective-permute-start.4 = (f32[16,48,128]{2,1,0:T(8,128)S(1)}, f32[16,48,128]{2,1,0:T(8,128)S(1)}, u32[]{:S(2)}, u32[]{:S(2)}) collective-permute-start(f32[16,48,128]{2,1,0:T(8,128)S(1)} %collective-permute-done.refs_1_), channel_id=1, source_target_pairs={{0,32},{32,0},{64,96},{96,64},{1,33},{33,1},{65,97},{97,65},{2,34}... | collective-permute-start | bytes 1179656 | tf_op jit(solution)/shard_map/ppermute | solution.py:385
  47.4 11.5 %collective-permute-start.1 = (f32[16,48,128]{2,1,0:T(8,128)S(1)}, f32[16,48,128]{2,1,0:T(8,128)S(1)}, u32[]{:S(2)}, u32[]{:S(2)}) collective-permute-start(f32[16,48,128]{2,1,0:T(8,128)S(1)} %collective-permute-done.refs_1_), channel_id=1, source_target_pairs={{0,64},{32,96},{64,0},{96,32},{1,65},{33,97},{65,1},{97,33},{2,66}... | collective-permute-start | bytes 1179656 | tf_op jit(solution)/shard_map/ppermute | solution.py:385
  59.0 1.7 %collective-permute-start.6 = (f32[16,48,128]{2,1,0:T(8,128)S(1)}, f32[16,48,128]{2,1,0:T(8,128)S(1)}, u32[]{:S(2)}, u32[]{:S(2)}) collective-permute-start(f32[16,48,128]{2,1,0:T(8,128)S(1)} %collective-permute-done.1.refs_0_), channel_id=1, source_target_pairs={{0,32},{32,0},{64,96},{96,64},{1,33},{33,1},{65,97},{97,65},{2,34}... | collective-permute-start | bytes 1179656 | tf_op jit(solution)/shard_map/ppermute | solution.py:385
  60.3 10.3 %copy-start.6 = (f32[2000]{0:T(1024)S(1)}, f32[2000]{0:T(1024)}, u32[]{:S(2)}) copy-start(f32[2000]{0:T(1024)} %param.14) | copy-start | bytes 24004
  60.3 10.4 %copy-start.4 = (s32[512,2]{0,1:T(2,128)S(1)}, s32[512,2]{0,1:T(2,128)}, u32[]{:S(2)}) copy-start(s32[512,2]{0,1:T(2,128)} %param.12) | copy-start | bytes 12292
  60.4 22.6 %copy-start.2 = (s32[192,2]{0,1:T(2,128)S(1)}, s32[192,2]{0,1:T(2,128)}, u32[]{:S(2)}) copy-start(s32[192,2]{0,1:T(2,128)} %param.10) | copy-start | bytes 4612
  60.4 22.6 %copy-start.5 = (f32[250]{0:T(256)S(1)}, f32[250]{0:T(256)}, u32[]{:S(2)}) copy-start(f32[250]{0:T(256)} %occupied_ref.1) | copy-start | bytes 3004
  62.8 20.1 %all-to-all-start.1 = ((f32[32,24,128]{2,1,0:T(8,128)}), f32[32,24,128]{2,1,0:T(8,128)S(1)}, u32[]{:S(2)}, u32[]{:S(2)}) async-start(f32[32,24,128]{2,1,0:T(8,128)} %bitcast.10), calls=%async_computation.1 | async-start | bytes 786432 | tf_op jit(solution)/shard_map/all_to_all | solution.py:422
